TPU v7x, 32 devices: a whole 2x2x4 slice. The times are simulated.
32 devices in a mesh: groups: 2 (over y), batch: 16 (over z, x, core).
Axes of the slice: x: 2, y: 2, z: 4, core: 2. Of those that a mesh axis runs over, the one named last changes fastest.
Arguments:
- queries: bfloat16 [64, 34, 8192], P(('groups', 'batch')), parts along dimension 0, may hold values from -6 to 6
- key_vectors: bfloat16 [64, 34, 8192], P(('groups', 'batch')), parts along dimension 0, may hold values from -0.5 to 0.5
- values: bfloat16 [64, 34, 8192], P(('groups', 'batch')), parts along dimension 0, may hold values from -6 to 6
- gate_logits: bfloat16 [64, 34, 8192], P(('groups', 'batch')), parts along dimension 0, may hold values from -6 to 6
- decay_rates: float32 [64], replicated, may hold values from 0.003 to 0.08
- norm_gain: float32 [8192], replicated, may hold values from 0.1 to 1.9
- pool_states: bfloat16 [32, 8192, 128], P(('groups', 'batch')), parts along dimension 0, may hold values from -1.75 to 1.75
- pool_entry: int32 [64], P(('groups', 'batch')), parts along dimension 0, may hold values from 0 to 15
Outputs:
- mixed: bfloat16 [64, 34, 8192], P(('groups', 'batch')), parts along dimension 0
- new_states: bfloat16 [64, 8192, 128], P('groups', 'batch'), parts along dimension 0
There are 2 independent parts, one for each index of `groups`. A program takes and returns all parts, laid end to end along the dimension named above; an argument that names none is the same for every part. Nothing has to cross between parts.
Inputs may be any that keep to these rules, and one draw needn't show every extreme that they name: `pool_entry`: entry e is the only entry of the pool shard on batch device e; several requests may name the same entry.
All inputs are finite; a program needn't handle non-finite values.
Results may differ from a plain program's by a relative error of at most 0.001.
Values may be sent and summed in bfloat16 or wider, within the bound.
No kernel may reach another device: no remote copies, remote signals or barrier semaphores. Data moves between devices by JAX's collectives and lax.ppermute only.
A program may use at most 64 MiB of HBM per device.

v0:
```python
import jax
import jax.numpy as jnp
from jax import lax
from jax.sharding import PartitionSpec as P


def finish_output(attended, gate_logits, norm_gain):
    mean_square = jnp.mean(attended * attended, axis=-1, keepdims=True)
    scaled = attended * lax.rsqrt(mean_square + 1e-05) * norm_gain
    return (scaled * jax.nn.sigmoid(gate_logits.astype(jnp.float32))).astype(jnp.bfloat16)


def attend(query_part, key_part, value_part, resumed, rates_here):
    length = query_part.shape[1]
    highest = lax.Precision.HIGHEST
    positions = jnp.arange(1, length + 1).astype(jnp.float32)
    decay_now = jnp.exp(-positions[:, None] * rates_here[None, :])
    from_state = jnp.einsum(
        "rtgd,rgde->rtge", query_part, resumed, preferred_element_type=jnp.float32
    )
    from_state = from_state * decay_now[None, :, :, None]
    key_wide = key_part.astype(jnp.float32)
    value_wide = value_part.astype(jnp.float32)
    distance = positions[:, None] - positions[None, :]
    decay_pair = jnp.where(
        (distance >= 0.0)[:, :, None],
        jnp.exp(-jnp.maximum(distance, 0.0)[:, :, None] * rates_here),
        0.0,
    )
    scores = (
        jnp.einsum("rtgd,rsgd->rtsg", query_part, key_part, preferred_element_type=jnp.float32)
        * decay_pair[None]
    )
    in_block = jnp.einsum("rtsg,rsge->rtge", scores, value_wide, precision=highest)
    tail_decay = jnp.exp(-(float(length) - positions)[:, None] * rates_here[None, :])
    weighted_keys = key_wide * tail_decay[None, :, :, None]
    updated = jnp.exp(-float(length) * rates_here)[None, :, None, None] * resumed.astype(
        jnp.float32
    )
    updated = updated + jnp.einsum("rsgd,rsge->rgde", weighted_keys, value_wide, precision=highest)
    return (from_state + in_block, updated)


def on_device(
    queries, key_vectors, values, gate_logits, decay_rates, norm_gain, pool_states, pool_entry
):
    req_dev, length, feature_width = queries.shape
    head_count = decay_rates.shape[0]
    head_size = pool_states.shape[2]
    entries = lax.all_gather(pool_entry, "batch", axis=0, tiled=True)
    spread = lax.all_to_all(pool_states, "batch", split_axis=1, concat_axis=0, tiled=True)
    chosen = jnp.take(spread, entries, axis=0)
    resumed = lax.all_to_all(chosen, "batch", split_axis=0, concat_axis=1, tiled=True)
    resumed = resumed.reshape(req_dev, head_count, head_size, head_size)
    shaped = (req_dev, length, head_count, head_size)
    attended, updated = attend(
        queries.reshape(shaped),
        key_vectors.reshape(shaped),
        values.reshape(shaped),
        resumed,
        decay_rates,
    )
    attended = attended.reshape(req_dev, length, feature_width)
    local_states = updated.astype(jnp.bfloat16).reshape(req_dev, feature_width, head_size)
    new_states = lax.all_to_all(local_states, "batch", split_axis=1, concat_axis=0, tiled=True)
    mixed = finish_output(attended, gate_logits, norm_gain)
    return (mixed, new_states)


def solution(mesh):
    placed = (
        P(("groups", "batch"), None, None),
        P(("groups", "batch"), None, None),
        P(("groups", "batch"), None, None),
        P(("groups", "batch"), None, None),
        P(),
        P(),
        P(("groups", "batch"), None, None),
        P(("groups", "batch")),
    )
    return jax.shard_map(
        on_device,
        mesh=mesh,
        in_specs=placed,
        out_specs=(P(("groups", "batch"), None, None), P("groups", "batch", None)),
        check_vma=False,
    )
```

profile of v0, /device:TPU:11, one launch (start us, length us, event | category | flops | bytes accessed | tf_op | source)
XLA Modules:
  0.0 375.3 jit_solution(9554630048918124368)
XLA Ops:
  0.6 7.5 %copy.67 = bf16[1,8192,128]{2,0,1:T(2,128)(2,1)} copy(bf16[1,8192,128]{2,1,0:T(8,128)(2,1)} %param.14) | data formatting | bytes 4194304 | tf_op args[6]
  8.1 0.5 broadcast.157
  8.6 45.2 %reduce.1 = bf16[8192,128]{1,0:T(8,128)(2,1)S(1)} reduce(bf16[8192,1,128]{2,1,0:T(2,128)(2,1)} %bitcast.38, bf16[]{:T(256)} %broadcast.157), dimensions={1}, to_apply=%bitcast.34.reduce_sub_computation | reduce | bytes 4194306
  53.8 2.0 reshape.201
  55.8 0.0 copy-start.7
  55.8 0.0 copy-start.6
  55.8 6.7 %all-to-all-start = ((bf16[16,2,32768]{2,1,0:T(2,128)(2,1)}), bf16[16,2,32768]{2,1,0:T(2,128)(2,1)S(1)}, u32[]{:S(2)}, u32[]{:S(2)}) async-start(bf16[16,2,32768]{2,1,0:T(2,128)(2,1)} %reshape.201), calls=%async_computation | async-start | bytes 4194304 | tf_op jit(solution)/shard_map/all_to_all | solution.py:51
  62.5 0.0 copy-done.7
  62.5 0.6 dynamic-slice
  63.7 0.0 copy-done.6
  63.7 0.2 dynamic-update-slice
  64.0 43.8 %all-reduce = s32[32]{0:T(128)S(1)} all-reduce(s32[32]{0:T(128)S(1)} %dynamic-update-slice), channel_id=1, replica_groups=mesh['groups'=2,'batch'=16] {'batch'}, use_global_device_ids=true, to_apply=%add | all-reduce | flops 32 | bytes 256
  107.8 2.2 all-to-all-done
  110.0 6.7 %reshape.202 = bf16[8192,1,128]{2,1,0:T(2,128)(2,1)} reshape(bf16[16,2,32768]{2,1,0:T(2,128)(2,1)S(1)} %all-to-all-done) | data formatting | bytes 4194304
  116.7 2.5 copy.49
  119.2 3.1 gather_fusion
  122.3 4.7 %broadcast_select_fusion = bf16[32,512,128]{2,1,0:T(8,128)(2,1)} fusion(bf16[32,512,128]{2,1,0:T(8,128)(2,1)} %gather_fusion, pred[32]{0:T(512)(128)(4,1)S(1)} %compare_and_fusion), kind=kLoop, calls=%fused_computation.2 | loop fusion | flops 2097152 | bytes 8388640 | tf_op jit(solution)/shard_map/jit(_take)/select_n | solution.py:52
  126.9 0.0 copy-start.2
  126.9 6.2 %all-to-all-start.1 = ((bf16[32,512,128]{2,1,0:T(8,128)(2,1)}), bf16[32,512,128]{2,1,0:T(8,128)(2,1)}, u32[]{:S(2)}, u32[]{:S(2)}) async-start(bf16[32,512,128]{2,1,0:T(8,128)(2,1)} %broadcast_select_fusion), calls=%async_computation.1 | async-start | bytes 8388608 | tf_op jit(solution)/shard_map/all_to_all | solution.py:53
  133.2 0.0 copy-done.2
  133.2 0.0 copy-start.5
  133.2 0.9 reshape.183
  134.1 3.2 reshape.184
  137.3 0.0 copy-done.5
  137.3 0.1 multiply_exponential_fusion
  137.4 88.3 %all-to-all-done.1 = bf16[32,512,128]{2,1,0:T(8,128)(2,1)} async-done(((bf16[32,512,128]{2,1,0:T(8,128)(2,1)}), bf16[32,512,128]{2,1,0:T(8,128)(2,1)}, u32[]{:S(2)}, u32[]{:S(2)}) %all-to-all-start.1) | async-done | bytes 4194336 | tf_op jit(solution)/shard_map/all_to_all | solution.py:53
  225.7 2.6 copy.36
  228.3 0.0 copy-start
  228.3 9.0 %add_convert_fusion = bf16[2,64,128,128]{3,2,1,0:T(8,128)(2,1)S(1)} fusion(bf16[2,64,128,128]{3,2,1,0:T(8,128)(2,1)S(1)} %bitcast.35, f32[64]{0:T(128)S(1)} %multiply_exponential_fusion.2, f32[34,64]{0,1:T(8,128)S(1)} %get-tuple-element.2, bf16[2,34,64,128]{3,2,0,1:T(8,128)(2,1)S(1)} %reshape.184, bf16[2,34,64,128]{3,2,0,1:T(8,128)(2,1)S(1)} %reshape.183), kind=kOutput, calls=%fused_computation.1 | convolution fusion | flops 865140736 | bytes 10625792 | tf_op jit(solution)/shard_map/rsgd,rsge->rgde/dot_general | solution.py:40
  237.3 0.0 copy-done
  237.3 35.5 %copy.46 = bf16[2,8192,128]{2,0,1:T(2,128)(2,1)} copy(bf16[2,8192,128]{2,1,0:T(8,128)(2,1)S(1)} %bitcast.40) | data formatting | bytes 8388608 | tf_op jit(solution)/shard_map/reshape | solution.py:64
  272.8 4.8 %all-to-all-start.2 = ((bf16[2,8192,128]{2,0,1:T(2,128)(2,1)}), bf16[2,8192,128]{2,0,1:T(2,128)(2,1)}, u32[]{:S(2)}, u32[]{:S(2)}) async-start(bf16[2,8192,128]{2,0,1:T(2,128)(2,1)} %copy.46), calls=%async_computation.2 | async-start | bytes 8388608 | tf_op jit(solution)/shard_map/all_to_all | solution.py:65
  277.6 3.2 reshape.182
  280.8 0.1 subtract_compare_fusion
  280.8 0.1 fusion.13
  280.9 0.2 exponential_select_fusion
  281.2 1.6 fusion.9
  282.7 0.0 copy-start.1
  282.7 3.1 fusion
  285.9 0.0 copy-done.1
  285.9 1.8 multiply_reduce_fusion
  287.6 1.8 copy.42
  289.4 0.0 copy-start.3
  289.4 0.0 copy-start.4
  289.4 2.9 reshape.185
  292.4 0.1 copy.43
  292.5 0.0 copy-done.3
  292.5 0.0 copy-done.4
  292.5 3.5 fusion.3
  296.0 74.1 %all-to-all-done.2 = bf16[2,8192,128]{2,0,1:T(2,128)(2,1)} async-done(((bf16[2,8192,128]{2,0,1:T(2,128)(2,1)}), bf16[2,8192,128]{2,0,1:T(2,128)(2,1)}, u32[]{:S(2)}, u32[]{:S(2)}) %all-to-all-start.2) | async-done | bytes 4194336 | tf_op jit(solution)/shard_map/all_to_all | solution.py:65
  370.1 5.2 %copy.47 = bf16[16,2,512,128]{3,2,1,0:T(8,128)(2,1)} copy(bf16[16,2,512,128]{3,1,2,0:T(2,128)(2,1)} %bitcast.9) | data formatting | bytes 8388608 | tf_op jit(solution)/shard_map/all_to_all | solution.py:65
  (8 shorter events, 0.0 us)
Async XLA Ops:
  55.8 6.7 %copy-start.7 = (u32[32]{0:T(128)S(1)}, u32[32]{0:T(128)}, u32[]{:S(2)}) copy-start(u32[32]{0:T(128)} %constant.40) | copy-start | bytes 388
  55.8 7.9 %copy-start.6 = (s32[2]{0:T(128)S(1)}, s32[2]{0:T(128)}, u32[]{:S(2)}) copy-start(s32[2]{0:T(128)} %param.15) | copy-start | bytes 28
  55.8 54.2 %all-to-all-start = ((bf16[16,2,32768]{2,1,0:T(2,128)(2,1)}), bf16[16,2,32768]{2,1,0:T(2,128)(2,1)S(1)}, u32[]{:S(2)}, u32[]{:S(2)}) async-start(bf16[16,2,32768]{2,1,0:T(2,128)(2,1)} %reshape.201), calls=%async_computation | async-start | bytes 4194304 | tf_op jit(solution)/shard_map/all_to_all | solution.py:51
  126.9 6.3 %copy-start.2 = (bf16[2,34,8192]{2,0,1:T(2,128)(2,1)S(1)}, bf16[2,34,8192]{2,0,1:T(2,128)(2,1)}, u32[]{:S(2)}) copy-start(bf16[2,34,8192]{2,0,1:T(2,128)(2,1)} %param.9) | copy-start | bytes 3342340
  126.9 98.7 %all-to-all-start.1 = ((bf16[32,512,128]{2,1,0:T(8,128)(2,1)}), bf16[32,512,128]{2,1,0:T(8,128)(2,1)}, u32[]{:S(2)}, u32[]{:S(2)}) async-start(bf16[32,512,128]{2,1,0:T(8,128)(2,1)} %broadcast_select_fusion), calls=%async_computation.1 | async-start | bytes 8388608 | tf_op jit(solution)/shard_map/all_to_all | solution.py:53
  133.2 4.1 %copy-start.5 = (f32[64]{0:T(128)S(1)}, f32[64]{0:T(128)}, u32[]{:S(2)}) copy-start(f32[64]{0:T(128)} %param.12) | copy-start | bytes 772
  228.3 9.0 %copy-start = (bf16[2,16,512,128]{3,2,1,0:T(8,128)(2,1)}, bf16[2,16,512,128]{3,2,1,0:T(8,128)(2,1)S(1)}, u32[]{:S(2)}) copy-start(bf16[2,16,512,128]{3,2,1,0:T(8,128)(2,1)S(1)} %copy.36) | copy-start | bytes 12582916
  272.8 97.2 %all-to-all-start.2 = ((bf16[2,8192,128]{2,0,1:T(2,128)(2,1)}), bf16[2,8192,128]{2,0,1:T(2,128)(2,1)}, u32[]{:S(2)}, u32[]{:S(2)}) async-start(bf16[2,8192,128]{2,0,1:T(2,128)(2,1)} %copy.46), calls=%async_computation.2 | async-start | bytes 8388608 | tf_op jit(solution)/shard_map/all_to_all | solution.py:65
  282.7 3.1 copy-start.1
  289.4 3.1 copy-start.3
  289.4 3.1 copy-start.4
where the time goes:
time: 376 us; the launch traced here: 375 us
  waiting for transfers between devices  165 us (44%)
  local copies, waits for them, and re-layouts  78.4 us (21%)
  other arithmetic  53.9 us (14%)
  blocking collectives  43.8 us (12%)
  starting transfers between devices  17.7 us (5%)
  matrix products  15.4 us (4%)
    all_to_all x1, waiting for transfers between devices, on_device(): lax.all_to_all(chosen, 'batch', split_axis=0, concat_axis=1, tiled=True)  88.3 us
    all_to_all x1, waiting for transfers between devices, on_device(): lax.all_to_all(local_states, 'batch', split_axis=1, concat_axis=0, tiled=...  74.1 us
    unnamed x1, other arithmetic  45.2 us
    unnamed x1, blocking collectives  43.8 us
    reshape x1, local copies, waits for them, and re-layouts, on_device(): updated.astype(jnp.bfloat16).reshape(req_dev, feature_width, head_size)  35.5 us
    unnamed x24, local copies, waits for them, and re-layouts  20 us
    dot_general x1, matrix products, attend(): jnp.einsum('rsgd,rsge->rgde', weighted_keys, value_wide, precision=highest)  8.99 us
  transfers between devices with their start and end apart: 3, of which 3 were waited for; matrix products, arithmetic and copies ran while one was open for 6% of the time, Pallas kernels for 0%

commit v1 on v0

--- a/solution.py
+++ b/solution.py
@@ -62,7 +62,12 @@
     )
     attended = attended.reshape(req_dev, length, feature_width)
     local_states = updated.astype(jnp.bfloat16).reshape(req_dev, feature_width, head_size)
-    new_states = lax.all_to_all(local_states, "batch", split_axis=1, concat_axis=0, tiled=True)
+    new_states = jnp.concatenate(
+        lax.all_to_all(
+            jnp.stack(jnp.split(local_states, lax.axis_size("batch"), axis=1)), "batch", 0, 0
+        ),
+        axis=0,
+    )
     mixed = finish_output(attended, gate_logits, norm_gain)
     return (mixed, new_states)
 

time: 376 us -> 351 us (0.934)
  local copies, waits for them, and re-layouts: 78.4 us -> 53.9 us
    reshape x1 -> x0, local copies, waits for them, and re-layouts: 35.5 us -> none  [on_device(): updated.astype(jnp.bfloat16).reshape(req_dev, feature_width, head_size)]
    unnamed x24 -> x40, local copies, waits for them, and re-layouts: 20 us -> 35.5 us
    all_to_all x1 -> x0, local copies, waits for them, and re-layouts: 5.21 us -> none  [on_device(): lax.all_to_all(local_states, 'batch', split_axis=1, concat_axis=0, tiled=...]
  transfers between devices with their start and end apart: 3 -> 3, of which waited for: 3 -> 3; matrix products, arithmetic and copies ran while one was open for 6% -> 7% of each run, Pallas kernels for 0% -> 0%
where the time goes in v1:
time: 351 us
  waiting for transfers between devices  165 us (47%)
  local copies, waits for them, and re-layouts  53.9 us (15%)
  other arithmetic  53.9 us (15%)
  blocking collectives  43.8 us (12%)
  starting transfers between devices  17.5 us (5%)
  matrix products  15.4 us (4%)
    all_to_all x1, waiting for transfers between devices, on_device(): lax.all_to_all(chosen, 'batch', split_axis=0, concat_axis=1, tiled=True)  88.3 us
    all_to_all x1, waiting for transfers between devices, on_device(): lax.all_to_all(jnp.stack(jnp.split(local_states, lax.axis_size('batch'),...  74.1 us
    unnamed x1, other arithmetic  45.2 us
    unnamed x1, blocking collectives  43.8 us
    unnamed x40, local copies, waits for them, and re-layouts  35.5 us
    dot_general x1, matrix products, attend(): jnp.einsum('rsgd,rsge->rgde', weighted_keys, value_wide, precision=highest)  8.99 us
  transfers between devices with their start and end apart: 3, of which 3 were waited for; matrix products, arithmetic and copies ran while one was open for 7% of the time, Pallas kernels for 0%

profile of v1, /device:TPU:11, one launch (start us, length us, event | category | flops | bytes accessed | tf_op | source)
XLA Modules:
  0.0 350.7 jit_solution(6221129569897583370)
XLA Ops:
  0.6 7.5 %copy.61 = bf16[1,8192,128]{2,0,1:T(2,128)(2,1)} copy(bf16[1,8192,128]{2,1,0:T(8,128)(2,1)} %param.14) | data formatting | bytes 4194304 | tf_op args[6]
  8.1 0.5 broadcast.157
  8.6 45.2 %reduce.1 = bf16[8192,128]{1,0:T(8,128)(2,1)S(1)} reduce(bf16[8192,1,128]{2,1,0:T(2,128)(2,1)} %bitcast.115, bf16[]{:T(256)} %broadcast.157), dimensions={1}, to_apply=%bitcast.95.reduce_sub_computation | reduce | bytes 4194306
  53.8 0.0 copy-start.7
  53.8 0.0 copy-start.6
  53.8 2.0 reshape.205
  55.8 6.5 %all-to-all-start = ((bf16[16,2,32768]{2,1,0:T(2,128)(2,1)}), bf16[16,2,32768]{2,1,0:T(2,128)(2,1)S(1)}, u32[]{:S(2)}, u32[]{:S(2)}) async-start(bf16[16,2,32768]{2,1,0:T(2,128)(2,1)} %reshape.205), calls=%async_computation | async-start | bytes 4194304 | tf_op jit(solution)/shard_map/all_to_all | solution.py:51
  62.3 0.0 copy-done.7
  62.3 0.6 dynamic-slice
  63.6 0.0 copy-done.6
  63.6 0.2 dynamic-update-slice
  63.8 43.8 %all-reduce = s32[32]{0:T(128)S(1)} all-reduce(s32[32]{0:T(128)S(1)} %dynamic-update-slice), channel_id=1, replica_groups=mesh['groups'=2,'batch'=16] {'batch'}, use_global_device_ids=true, to_apply=%add | all-reduce | flops 32 | bytes 256
  107.7 2.2 all-to-all-done
  109.9 6.7 %reshape.206 = bf16[8192,1,128]{2,1,0:T(2,128)(2,1)} reshape(bf16[16,2,32768]{2,1,0:T(2,128)(2,1)S(1)} %all-to-all-done) | data formatting | bytes 4194304
  116.6 2.5 copy.43
  119.1 3.1 gather_fusion
  122.2 4.7 %broadcast_select_fusion = bf16[32,512,128]{2,1,0:T(8,128)(2,1)} fusion(bf16[32,512,128]{2,1,0:T(8,128)(2,1)} %gather_fusion, pred[32]{0:T(512)(128)(4,1)S(1)} %compare_and_fusion), kind=kLoop, calls=%fused_computation.2 | loop fusion | flops 2097152 | bytes 8388640 | tf_op jit(solution)/shard_map/jit(_take)/select_n | solution.py:52
  126.8 0.0 copy-start.2
  126.8 6.2 %all-to-all-start.1 = ((bf16[32,512,128]{2,1,0:T(8,128)(2,1)}), bf16[32,512,128]{2,1,0:T(8,128)(2,1)}, u32[]{:S(2)}, u32[]{:S(2)}) async-start(bf16[32,512,128]{2,1,0:T(8,128)(2,1)} %broadcast_select_fusion), calls=%async_computation.1 | async-start | bytes 8388608 | tf_op jit(solution)/shard_map/all_to_all | solution.py:53
  133.1 0.0 copy-done.2
  133.1 0.0 copy-start.5
  133.1 0.9 reshape.186
  134.0 3.2 reshape.187
  137.2 0.0 copy-done.5
  137.2 0.1 multiply_exponential_fusion
  137.3 88.3 %all-to-all-done.1 = bf16[32,512,128]{2,1,0:T(8,128)(2,1)} async-done(((bf16[32,512,128]{2,1,0:T(8,128)(2,1)}), bf16[32,512,128]{2,1,0:T(8,128)(2,1)}, u32[]{:S(2)}, u32[]{:S(2)}) %all-to-all-start.1) | async-done | bytes 4194336 | tf_op jit(solution)/shard_map/all_to_all | solution.py:53
  225.6 2.6 copy.32
  228.2 0.0 copy-start
  228.2 9.0 %add_convert_fusion = bf16[2,64,128,128]{3,2,1,0:T(8,128)(2,1)S(1)} fusion(bf16[2,64,128,128]{3,2,1,0:T(8,128)(2,1)S(1)} %bitcast.96, f32[64]{0:T(128)S(1)} %multiply_exponential_fusion.2, f32[34,64]{0,1:T(8,128)S(1)} %get-tuple-element.2, bf16[2,34,64,128]{3,2,0,1:T(8,128)(2,1)S(1)} %reshape.187, bf16[2,34,64,128]{3,2,0,1:T(8,128)(2,1)S(1)} %reshape.186), kind=kOutput, calls=%fused_computation.1 | convolution fusion | flops 865140736 | bytes 10625792 | tf_op jit(solution)/shard_map/rsgd,rsge->rgde/dot_general | solution.py:40
  237.2 0.0 copy-done
  237.2 0.7 fusion.28
  238.0 0.7 fusion.27
  238.7 0.7 fusion.26
  239.4 0.7 fusion.25
  240.1 0.7 fusion.24
  240.9 0.7 fusion.23
  241.6 0.7 fusion.22
  242.3 0.7 fusion.21
  243.0 0.7 fusion.20
  243.8 0.7 fusion.19
  244.5 0.7 fusion.18
  245.2 0.7 fusion.17
  245.9 0.7 fusion.16
  246.7 0.7 fusion.15
  247.4 0.7 fusion.14
  248.1 0.8 fusion.13
  248.9 4.8 %all-to-all-start.2 = ((bf16[16,2,512,128]{3,2,1,0:T(8,128)(2,1)}), bf16[16,2,512,128]{3,2,1,0:T(8,128)(2,1)}, u32[]{:S(2)}, u32[]{:S(2)}) async-start(bf16[16,2,512,128]{3,2,1,0:T(8,128)(2,1)} %fusion.13), calls=%async_computation.2 | async-start | bytes 8388608 | tf_op jit(solution)/shard_map/all_to_all | solution.py:66
  253.6 3.2 reshape.185
  256.8 0.1 subtract_compare_fusion
  256.9 0.1 fusion.29
  257.0 0.2 exponential_select_fusion
  257.2 1.6 fusion.9
  258.8 0.0 copy-start.1
  258.8 3.1 fusion
  261.9 0.0 copy-done.1
  261.9 1.8 multiply_reduce_fusion
  263.7 1.8 copy.38
  265.5 2.8 reshape.188
  268.3 0.1 copy.39
  268.4 0.0 copy-done.3
  268.4 0.0 copy-done.4
  268.4 3.5 %fusion.3 = bf16[2,34,8192]{2,0,1:T(2,128)(2,1)} fusion(bf16[2,34,8192]{2,0,1:T(2,128)(2,1)S(1)} %copy-done.3, f32[2,34,8192]{2,0,1:T(2,128)S(1)} %reshape.188, f32[8192]{0:T(1024)S(1)} %copy-done.4, f32[2,34]{0,1:T(8,128)S(1)} %copy.39), kind=kLoop, calls=%fused_computation.11 | loop fusion | flops 4456448 | bytes 4489488 | tf_op jit(solution)/shard_map/convert_element_type | solution.py:10
  271.9 74.1 %all-to-all-done.2 = bf16[16,2,512,128]{3,2,1,0:T(8,128)(2,1)} async-done(((bf16[16,2,512,128]{3,2,1,0:T(8,128)(2,1)}), bf16[16,2,512,128]{3,2,1,0:T(8,128)(2,1)}, u32[]{:S(2)}, u32[]{:S(2)}) %all-to-all-start.2) | async-done | bytes 4194336 | tf_op jit(solution)/shard_map/all_to_all | solution.py:66
  346.1 4.7 %copy.79 = bf16[32,512,128]{2,1,0:T(8,128)(2,1)} copy(bf16[32,512,128]{2,1,0:T(8,128)(2,1)} %bitcast.24) | data formatting | bytes 8388608
  (10 shorter events, 0.1 us)
Async XLA Ops:
  53.8 8.6 %copy-start.7 = (u32[32]{0:T(128)S(1)}, u32[32]{0:T(128)}, u32[]{:S(2)}) copy-start(u32[32]{0:T(128)} %constant.40) | copy-start | bytes 388
  53.8 9.8 %copy-start.6 = (s32[2]{0:T(128)S(1)}, s32[2]{0:T(128)}, u32[]{:S(2)}) copy-start(s32[2]{0:T(128)} %param.15) | copy-start | bytes 28
  55.8 54.1 %all-to-all-start = ((bf16[16,2,32768]{2,1,0:T(2,128)(2,1)}), bf16[16,2,32768]{2,1,0:T(2,128)(2,1)S(1)}, u32[]{:S(2)}, u32[]{:S(2)}) async-start(bf16[16,2,32768]{2,1,0:T(2,128)(2,1)} %reshape.205), calls=%async_computation | async-start | bytes 4194304 | tf_op jit(solution)/shard_map/all_to_all | solution.py:51
  126.8 6.3 %copy-start.2 = (bf16[2,34,8192]{2,0,1:T(2,128)(2,1)S(1)}, bf16[2,34,8192]{2,0,1:T(2,128)(2,1)}, u32[]{:S(2)}) copy-start(bf16[2,34,8192]{2,0,1:T(2,128)(2,1)} %param.9) | copy-start | bytes 3342340
  126.8 98.7 %all-to-all-start.1 = ((bf16[32,512,128]{2,1,0:T(8,128)(2,1)}), bf16[32,512,128]{2,1,0:T(8,128)(2,1)}, u32[]{:S(2)}, u32[]{:S(2)}) async-start(bf16[32,512,128]{2,1,0:T(8,128)(2,1)} %broadcast_select_fusion), calls=%async_computation.1 | async-start | bytes 8388608 | tf_op jit(solution)/shard_map/all_to_all | solution.py:53
  133.1 4.1 %copy-start.5 = (f32[64]{0:T(128)S(1)}, f32[64]{0:T(128)}, u32[]{:S(2)}) copy-start(f32[64]{0:T(128)} %param.12) | copy-start | bytes 772
  228.2 9.0 %copy-start = (bf16[2,16,512,128]{3,2,1,0:T(8,128)(2,1)}, bf16[2,16,512,128]{3,2,1,0:T(8,128)(2,1)S(1)}, u32[]{:S(2)}) copy-start(bf16[2,16,512,128]{3,2,1,0:T(8,128)(2,1)S(1)} %copy.32) | copy-start | bytes 12582916
  248.9 97.2 %all-to-all-start.2 = ((bf16[16,2,512,128]{3,2,1,0:T(8,128)(2,1)}), bf16[16,2,512,128]{3,2,1,0:T(8,128)(2,1)}, u32[]{:S(2)}, u32[]{:S(2)}) async-start(bf16[16,2,512,128]{3,2,1,0:T(8,128)(2,1)} %fusion.13), calls=%async_computation.2 | async-start | bytes 8388608 | tf_op jit(solution)/shard_map/all_to_all | solution.py:66
  258.8 3.1 copy-start.1
  263.7 4.7 %copy-start.3 = (bf16[2,34,8192]{2,0,1:T(2,128)(2,1)S(1)}, bf16[2,34,8192]{2,0,1:T(2,128)(2,1)}, u32[]{:S(2)}) copy-start(bf16[2,34,8192]{2,0,1:T(2,128)(2,1)} %param.11) | copy-start | bytes 3342340
  263.7 4.7 %copy-start.4 = (f32[8192]{0:T(1024)S(1)}, f32[8192]{0:T(1024)}, u32[]{:S(2)}) copy-start(f32[8192]{0:T(1024)} %param.13) | copy-start | bytes 98308
